TPU v7x, 32 devices: a whole 2x2x4 slice. The times are simulated.
32 devices in a mesh: ctx: 16 (over z, y, core), sec: 2 (over x).
Axes of the slice: x: 2, y: 2, z: 4, core: 2. Of those that a mesh axis runs over, the one named last changes fastest.
Arguments:
- query_nope: bfloat16 [1024, 8192], P('ctx', 'sec'), may hold values from -6 to 6
- query_rope: bfloat16 [1024, 4096], P('ctx', 'sec'), may hold values from -8 to 8
- key_latent: bfloat16 [1024, 512], P('ctx'), may hold values from -6 to 6
- key_rope: bfloat16 [1024, 64], P('ctx'), may hold values from -8 to 8
- key_up: bfloat16 [64, 512, 128], P('sec'), may hold values from -0.25 to 0.25
- value_up: bfloat16 [64, 512, 128], P('sec'), may hold values from -1 to 1
- routed_tokens: bfloat16 [4096, 7168], P(('ctx', 'sec')), may hold values from -6 to 6
- expert_ids: int32 [4096, 8], P(('ctx', 'sec')), may hold values from 0 to 255, as said below
- expert_gates: float32 [4096, 8], P(('ctx', 'sec')), may hold values from 0.2 to 2
- gate_weight: bfloat16 [7168, 8192], P(None, ('ctx', 'sec')), may hold values from -0.0625 to 0.0625
- up_weight: bfloat16 [7168, 8192], P(None, ('ctx', 'sec')), may hold values from -0.0625 to 0.0625
- down_weight: bfloat16 [8192, 7168], P(('ctx', 'sec')), may hold values from -0.125 to 0.125
Outputs:
- attention_out: bfloat16 [1024, 8192], P('ctx', 'sec')
- routed_out: bfloat16 [4096, 7168], P(('ctx', 'sec'))
Inputs may be any that keep to these rules, and one draw needn't show every extreme that they name: `expert_ids`: each row names 8 different experts, at most one of them below 4. Within each aligned block of 128 rows (the rows of one device) no expert below 4 is named more than 4 times, and in every draw one expert below 4 is named exactly 4 times in every block.
All inputs are finite; a program needn't handle non-finite values.
Results may differ from a plain program's by a relative error of at most 0.008.
Values may be sent and summed in bfloat16 or wider, within the bound.
A program may use at most 192 MiB of HBM per device.

v0:
```python
import jax
import jax.numpy as jnp
from jax import lax
from jax.sharding import PartitionSpec as P

ROPE = 64
NOPE = 128
SPLIT = 8
CAP = 4


masked_score = -1e30


def swapped(shard, axis, bit):
    return lax.ppermute(shard, axis, [(i, i ^ 1 << bit) for i in range(lax.axis_size(axis))])


def query_parts(nope_rows, rope_rows, key_up):
    row_count = nope_rows.shape[0]
    head_count = key_up.shape[0]
    nope_heads = nope_rows.reshape(row_count, head_count, -1)
    latents = jnp.einsum(
        "thn,hcn->thc", nope_heads, key_up, preferred_element_type=jnp.float32
    ).astype(jnp.bfloat16)
    return (latents, rope_rows.reshape(row_count, head_count, -1))


def attend_piece(running, latents, rotary, first_place, key_piece, key_start):
    latent_keys, rotary_keys = key_piece
    key_count = latent_keys.shape[0]
    unit_rows = latents.shape[0]

    def update(current):
        run_max, run_sum, weighted = current
        score_scale = (NOPE + ROPE) ** (-0.5)
        scores = jnp.einsum("uhc,pc->hup", latents, latent_keys, preferred_element_type=jnp.float32)
        scores = (
            scores
            + jnp.einsum("uhr,pr->hup", rotary, rotary_keys, preferred_element_type=jnp.float32)
        ) * score_scale
        key_place = jnp.arange(key_count, dtype=jnp.int32)
        query_place = first_place + jnp.arange(unit_rows, dtype=jnp.int32)
        allowed = key_place[None, None, :] <= query_place[None, :, None]
        scores = jnp.where(allowed, scores, masked_score)
        new_max = jnp.maximum(run_max, jnp.max(scores, axis=2))
        exponent = jnp.where(allowed, jnp.exp(scores - new_max[:, :, None]), 0.0)
        weights = exponent.astype(jnp.bfloat16)
        weighted = jnp.einsum(
            "hup,pc->huc", weights, latent_keys, preferred_element_type=jnp.float32
        )
        run_sum = jnp.sum(exponent, axis=2)
        return (new_max, run_sum, weighted)

    return lax.cond(
        key_start > first_place + unit_rows - 1, lambda current: current, update, running
    )


def finish_unit(running, value_up):
    run_max, run_sum, weighted = running
    latent_out = (weighted / run_sum[:, :, None]).astype(jnp.bfloat16)
    values = jnp.einsum("huc,hcv->uhv", latent_out, value_up, preferred_element_type=jnp.float32)
    return values.astype(jnp.bfloat16).reshape(values.shape[0], -1)


def attention(query_nope, query_rope, key_latent, key_rope, key_up, value_up):
    row_count = query_nope.shape[0]
    half_rows = row_count // 2
    cycle_index = lax.axis_index("ctx")
    front_place = cycle_index * row_count
    back_nope = query_nope[half_rows:]
    back_rope = query_rope[half_rows:]
    back_place = front_place + half_rows
    front_latent, front_rotary = query_parts(query_nope[:half_rows], query_rope[:half_rows], key_up)
    back_latent, back_rotary = query_parts(back_nope, back_rope, key_up)
    head_count = key_up.shape[0]
    latent_width = key_up.shape[1]
    initial = (
        jnp.full((head_count, half_rows), masked_score, jnp.float32),
        jnp.zeros((head_count, half_rows), jnp.float32),
        jnp.zeros((head_count, half_rows, latent_width), jnp.float32),
    )
    key_piece = (
        lax.all_gather(key_latent, "ctx", axis=0, tiled=True),
        lax.all_gather(key_rope, "ctx", axis=0, tiled=True),
    )
    key_start = jnp.int32(0)
    front_out = finish_unit(
        attend_piece(initial, front_latent, front_rotary, front_place, key_piece, key_start),
        value_up,
    )
    back_out = finish_unit(
        attend_piece(initial, back_latent, back_rotary, back_place, key_piece, key_start), value_up
    )
    return jnp.concatenate([front_out, back_out], axis=0)


def route_tables(expert_ids, expert_gates, round_experts):
    token_count, route_count = expert_ids.shape
    flattened = expert_ids.reshape(-1)
    matches = (flattened[:, None] == jnp.arange(round_experts, dtype=jnp.int32)[None, :]).astype(
        jnp.int32
    )
    earlier = jnp.cumsum(matches, axis=0) - matches
    slot_rank = jnp.sum(earlier * matches, axis=1)
    target = jnp.where(flattened < round_experts, flattened * CAP + slot_rank, -1)
    one_hot = target[:, None] == jnp.arange(round_experts * CAP, dtype=jnp.int32)[None, :]
    one_hot = one_hot.reshape(token_count, route_count, round_experts * CAP)
    selector = jnp.sum(one_hot.astype(jnp.float32), axis=1).astype(jnp.bfloat16)
    combine_weight = jnp.sum(jnp.where(one_hot, expert_gates[:, :, None], 0.0), axis=1)
    return (selector, combine_weight)


def expert_block(arrived, gate_weight, up_weight, down_weight):
    item_count = arrived.shape[1]
    flattened = arrived.reshape(-1, arrived.shape[2])
    gate_act = jnp.dot(flattened, gate_weight, preferred_element_type=jnp.float32)
    up_act = jnp.dot(flattened, up_weight, preferred_element_type=jnp.float32)
    hidden = (jax.nn.silu(gate_act) * up_act).astype(jnp.bfloat16)
    partial_value = jnp.dot(hidden, down_weight, preferred_element_type=jnp.float32)
    return partial_value.reshape(arrived.shape[0], item_count, -1)


def combine_back(partial_value, round_experts):
    item_count = partial_value.shape[1]
    model_width = partial_value.shape[2]
    returned = lax.all_to_all(
        partial_value.astype(jnp.bfloat16), ("ctx", "sec"), split_axis=0, concat_axis=0, tiled=True
    ).astype(partial_value.dtype)
    return jnp.sum(returned.reshape(round_experts, SPLIT, item_count, model_width), axis=1)


def experts_layer(routed_tokens, expert_ids, expert_gates, gate_weight, up_weight, down_weight):
    device_count = lax.axis_size("ctx") * lax.axis_size("sec")
    round_experts = device_count // SPLIT
    device_index = lax.axis_index(("ctx", "sec"))
    model_width = routed_tokens.shape[1]
    selector, combine_weight = route_tables(expert_ids, expert_gates, round_experts)
    outgoing = jnp.einsum(
        "ts,td->sd", selector, routed_tokens, preferred_element_type=jnp.float32
    ).astype(jnp.bfloat16)
    outgoing = outgoing.reshape(round_experts, CAP, model_width)
    block_width = model_width // SPLIT
    blocks = outgoing.reshape(round_experts, CAP, SPLIT, block_width).transpose(0, 2, 1, 3)
    blocks = blocks.reshape(device_count, CAP, block_width)
    arrived = lax.all_to_all(blocks, ("ctx", "sec"), split_axis=0, concat_axis=0, tiled=True)
    for bit_index in range(SPLIT.bit_length() - 1):
        partner = swapped(arrived, ("ctx", "sec"), bit_index)
        upper_bit = device_index >> bit_index & 1 == 1
        arrived = jnp.where(
            upper_bit,
            jnp.concatenate([partner, arrived], axis=2),
            jnp.concatenate([arrived, partner], axis=2),
        )
    results = combine_back(
        expert_block(arrived, gate_weight, up_weight, down_weight), round_experts
    )
    results = results.reshape(round_experts * CAP, model_width)
    mixed = jnp.dot(
        combine_weight, results, precision=lax.Precision.HIGHEST, preferred_element_type=jnp.float32
    )
    return mixed.astype(jnp.bfloat16)


def local(
    query_nope,
    query_rope,
    key_latent,
    key_rope,
    key_up,
    value_up,
    routed_tokens,
    expert_ids,
    expert_gates,
    gate_weight,
    up_weight,
    down_weight,
):
    attention_out = attention(query_nope, query_rope, key_latent, key_rope, key_up, value_up)
    routed_out = experts_layer(
        routed_tokens, expert_ids, expert_gates, gate_weight, up_weight, down_weight
    )
    return (attention_out, routed_out)


def solution(mesh):
    return jax.shard_map(
        local,
        mesh=mesh,
        in_specs=(
            P("ctx", "sec"),
            P("ctx", "sec"),
            P("ctx", None),
            P("ctx", None),
            P("sec", None, None),
            P("sec", None, None),
            P(("ctx", "sec"), None),
            P(("ctx", "sec"), None),
            P(("ctx", "sec"), None),
            P(None, ("ctx", "sec")),
            P(None, ("ctx", "sec")),
            P(("ctx", "sec"), None),
        ),
        out_specs=(P("ctx", "sec"), P(("ctx", "sec"), None)),
        check_vma=False,
    )
```

profile of v0, /device:TPU:11, one launch (start us, length us, event | category | flops | bytes accessed | tf_op | source)
XLA Modules:
  0.0 181.2 jit_solution(1728123941115606084)
XLA Ops:
  12.1 13.9 %all_to_all.10 = bf16[32,4,896]{2,1,0:T(4,128)(2,1)S(1)} all-to-all(bf16[32,4,896]{2,1,0:T(4,128)(2,1)S(1)} %copy.117), channel_id=1, replica_groups=mesh['ctx'=16,'sec'=2] {'ctx','sec'}, dimensions={0} | all-to-all | bytes 458752 | tf_op jit(solution)/shard_map/all_to_all | solution.py:147
  26.0 1.4 collective-permute-start
  27.4 5.2 %collective-permute-done = bf16[32,4,896]{2,1,0:T(4,128)(2,1)S(1)} collective-permute-done((bf16[32,4,896]{2,1,0:T(4,128)(2,1)S(1)}, bf16[32,4,896]{2,1,0:T(4,128)(2,1)S(1)}, u32[]{:S(2)}, u32[]{:S(2)}) %collective-permute-start) | collective-permute-done | bytes 229408 | tf_op jit(solution)/shard_map/ppermute | solution.py:16
  32.9 1.5 collective-permute-start.1
  34.4 1.4 collective-permute-done.1
  35.9 1.6 maximum_select_fusion.1
  39.7 20.3 %collective-permute-done.2 = bf16[32,4,3584]{2,1,0:T(4,128)(2,1)S(1)} collective-permute-done((bf16[32,4,3584]{2,1,0:T(4,128)(2,1)}, bf16[32,4,3584]{2,1,0:T(4,128)(2,1)S(1)}, u32[]{:S(2)}, u32[]{:S(2)}) %collective-permute-start.2) | collective-permute-done | bytes 917536 | tf_op jit(solution)/shard_map/ppermute | solution.py:16
  61.1 3.4 %fusion.24 = f32[128,256]{1,0:T(8,128)S(1)} fusion(bf16[7168,256]{1,0:T(8,128)(2,1)} %param.26, bf16[128,3584]{1,0:T(8,128)(2,1)} %maximum_select_fusion.2, bf16[128,3584]{1,0:T(8,128)(2,1)S(1)} %concatenate.48, pred[]{:T(512)S(6)} %eq.59), kind=kOutput, calls=%fused_computation.50 | convolution fusion | flops 478019584 | bytes 5636097 | tf_op jit(solution)/shard_map/dot_general | solution.py:119
  64.6 5.9 %convolution_convert_fusion.1 = bf16[128,7168]{1,0:T(8,128)(2,1)S(1)} fusion(bf16[256,7168]{1,0:T(8,128)(2,1)} %param.27, f32[128,256]{1,0:T(8,128)S(1)} %fusion.24, bf16[7168,256]{1,0:T(8,128)(2,1)} %param.25, bf16[128,3584]{1,0:T(8,128)(2,1)S(1)} %copy-done.6, bf16[128,3584]{1,0:T(8,128)(2,1)} %copy-done.5, pred[]{:T(512)S(6)} %eq.59), kind=kOutput, calls=%fused_computation.29 | convolution fusion | flops 948895744 | bytes 11141121 | tf_op jit(solution)/shard_map/dot_general | solution.py:121
  70.5 1.6 convert_element_type.91
  72.1 6.3 %all-to-all-start.1 = ((bf16[32,4,7168]{2,1,0:T(4,128)(2,1)}), bf16[32,4,7168]{2,1,0:T(4,128)(2,1)}, u32[]{:S(2)}, u32[]{:S(2)}) async-start(bf16[32,4,7168]{2,1,0:T(4,128)(2,1)} %convert_element_type.91), calls=%async_computation.1 | async-start | bytes 3670016 | tf_op jit(solution)/shard_map/all_to_all | solution.py:128
  78.5 52.8 %all_gather.7 = bf16[1024,64]{1,0:T(8,128)(2,1)S(1)} all-gather(bf16[64,64]{1,0:T(8,128)(2,1)S(1)} %copy-done.9), channel_id=1, replica_groups=mesh['ctx'=16,'sec'=2] {'ctx'}, dimensions={0}, use_global_device_ids=true | all-gather | bytes 139264 | tf_op jit(solution)/shard_map/all_gather | solution.py:86
  131.4 3.7 %fusion.19 = bf16[32,32,512]{2,0,1:T(8,128)(2,1)S(1)} fusion(bf16[32,512,128]{2,1,0:T(8,128)(2,1)} %param.20, bf16[4,32,8,128]{3,2,1,0:T(8,128)(2,1)S(1)} %get-tuple-element.127), kind=kOutput, calls=%fused_computation.38 | convolution fusion | flops 134742016 | bytes 5505024 | tf_op jit(solution)/shard_map/thn,hcn->thc/dot_general | solution.py:23
  135.1 1.5 fusion.18
  136.7 10.8 %conditional.3 = (f32[32,32]{0,1:T(8,128)S(1)}, f32[32,32,512]{2,1,0:T(8,128)S(1)}) conditional(s32[]{:T(128)} %convert_element_type.78, (s32[]{:T(128)}, bf16[1024,512]{1,0:T(8,128)(2,1)}, bf16[32,32,512]{2,0,1:T(8,128)(2,1)S(1)}, bf16[64,2048]{1,0:T(8,128)(2,1)S(1)}, bf16[1024,64]{1,0:T(8,128)(2,1)S(1)}) %tuple.57, () %tuple.30), branch_computations={%region_4.7_spmd, %region_7.8_spmd} | conditional | flops 2290121728 | bytes 31314236 | solution.py:55
  136.7 4.6 %fusion.14 = f32[1024,32,32]{0,2,1:T(8,128)} fusion(bf16[1024,512]{1,0:T(8,128)(2,1)} %get-tuple-element.42, bf16[32,32,512]{2,0,1:T(8,128)(2,1)S(1)} %get-tuple-element.113), kind=kOutput, calls=%fused_computation.21 | convolution fusion | flops 1073741824 | bytes 6291456 | tf_op jit(solution)/shard_map/cond/branch_0_fun/uhc,pc->hup/dot_general | solution.py:37
  141.7 3.2 %fusion.41 = (f32[32,32]{0,1:T(8,128)S(1)}, f32[32,32,1024]{2,0,1:T(8,128)S(1)}) fusion(f32[1024,32,32]{0,2,1:T(8,128)} %fusion.14, bf16[32,32,64]{2,1,0:T(8,128)(2,1)S(1)} %reshape.144, bf16[1024,64]{1,0:T(8,128)(2,1)S(1)} %get-tuple-element.115, pred[32,1024]{1,0:T(8,128)(4,1)S(1)} %iota_compare_fusion.1), kind=kOutput, calls=%fused_computation.81 | convolution fusion | flops 138411008 | bytes 8687616 | tf_op jit(solution)/shard_map/cond/branch_0_fun/uhr,pr->hup/dot_general | solution.py:40
  146.2 1.4 fusion.11
  148.9 10.8 %conditional.2 = (f32[32,32]{0,1:T(8,128)S(1)}, f32[32,32,512]{2,1,0:T(8,128)S(1)}) conditional(s32[]{:T(128)} %convert_element_type.72, (s32[]{:T(128)}, bf16[1024,512]{1,0:T(8,128)(2,1)}, bf16[32,32,512]{2,0,1:T(8,128)(2,1)S(1)}, bf16[64,2048]{1,0:T(8,128)(2,1)S(1)}, bf16[1024,64]{1,0:T(8,128)(2,1)S(1)}) %tuple.58, () %tuple.28), branch_computations={%region_0.3_spmd, %region_3.4_spmd} | conditional | flops 2290121728 | bytes 31314224 | solution.py:55
  148.9 4.6 %fusion.5 = f32[1024,32,32]{0,2,1:T(8,128)} fusion(bf16[1024,512]{1,0:T(8,128)(2,1)} %get-tuple-element.37, bf16[32,32,512]{2,0,1:T(8,128)(2,1)S(1)} %get-tuple-element.108), kind=kOutput, calls=%fused_computation.7 | convolution fusion | flops 1073741824 | bytes 6291456 | tf_op jit(solution)/shard_map/cond/branch_0_fun/uhc,pc->hup/dot_general | solution.py:37
  153.9 3.2 %fusion.40 = (f32[32,32]{0,1:T(8,128)S(1)}, f32[32,32,1024]{2,0,1:T(8,128)S(1)}) fusion(f32[1024,32,32]{0,2,1:T(8,128)} %fusion.5, bf16[32,32,64]{2,1,0:T(8,128)(2,1)S(1)} %reshape.143, bf16[1024,64]{1,0:T(8,128)(2,1)S(1)} %get-tuple-element.110, pred[32,1024]{1,0:T(8,128)(4,1)S(1)} %iota_compare_fusion), kind=kOutput, calls=%fused_computation.80 | convolution fusion | flops 138411008 | bytes 8687616 | tf_op jit(solution)/shard_map/cond/branch_0_fun/uhr,pr->hup/dot_general | solution.py:40
  161.2 3.9 %fusion.21 = bf16[32,4,8,128]{3,2,1,0:T(8,128)(2,1)S(1)} fusion(bf16[32,512,128]{2,1,0:T(8,128)(2,1)} %param.21, f32[32,32,512]{2,1,0:T(8,128)} %copy-done.11, f32[32,32]{1,0:T(8,128)S(1)} %copy.111), kind=kOutput, calls=%fused_computation.42 | convolution fusion | flops 135397376 | bytes 6557696 | tf_op jit(solution)/shard_map/huc,hcv->uhv/dot_general | solution.py:63
  167.5 2.4 %convert_reduce_fusion = f32[4,4,7168]{2,1,0:T(4,128)S(1)} fusion(bf16[32,4,7168]{2,1,0:T(4,128)(2,1)} %all-to-all-done.1), kind=kLoop, calls=%fused_computation.31 | loop fusion | flops 1720320 | bytes 2293760 | tf_op jit(solution)/shard_map/reduce_sum | solution.py:131
  170.1 4.2 %convolution_convert_fusion = bf16[128,7168]{1,0:T(8,128)(2,1)} fusion(f32[128,16]{0,1:T(8,128)S(1)} %get-tuple-element.117, f32[16,7168]{1,0:T(8,128)S(1)} %reshape.162), kind=kOutput, calls=%fused_computation.28 | convolution fusion | flops 177078272 | bytes 2301952 | tf_op jit(solution)/shard_map/dot_general | solution.py:160
  (77 shorter events, 18.4 us)
Async XLA Ops:
  7.2 4.4 %copy-start = (bf16[128,7168]{1,0:T(8,128)(2,1)S(1)}, bf16[128,7168]{1,0:T(8,128)(2,1)}, u32[]{:S(2)}) copy-start(bf16[128,7168]{1,0:T(8,128)(2,1)} %param.22) | copy-start | bytes 5505028
  7.2 129.5 %all-gather.2.cloned.1.call-start = ((), (), s32[]{:S(2)}) async-start(), calls=%async_computation.2 | async-start | bytes 1114112 | tf_op jit(solution)/shard_map/all_gather | solution.py:85
  26.0 6.6 %collective-permute-start = (bf16[32,4,896]{2,1,0:T(4,128)(2,1)S(1)}, bf16[32,4,896]{2,1,0:T(4,128)(2,1)S(1)}, u32[]{:S(2)}, u32[]{:S(2)}) collective-permute-start(bf16[32,4,896]{2,1,0:T(4,128)(2,1)S(1)} %all_to_all.10), channel_id=1, source_target_pairs={{0,1},{1,0},{2,3},{3,2},{4,5},{5,4},{6,7},{7,6},{8,9},{9,8},{10,11... | collective-permute-start | bytes 688136 | tf_op jit(solution)/shard_map/ppermute | solution.py:16
  32.9 3.0 %collective-permute-start.1 = (bf16[32,4,1792]{2,1,0:T(4,128)(2,1)S(1)}, bf16[32,4,1792]{2,1,0:T(4,128)(2,1)S(1)}, u32[]{:S(2)}, u32[]{:S(2)}) collective-permute-start(bf16[32,4,1792]{2,1,0:T(4,128)(2,1)S(1)} %maximum_select_fusion.3), channel_id=1, source_target_pairs={{0,2},{1,3},{2,0},{3,1},{4,6},{5,7},{6,4},{7,5},{8,10},{9,11},{10,... | collective-permute-start | bytes 1376264 | tf_op jit(solution)/shard_map/ppermute | solution.py:16
  37.5 22.4 %collective-permute-start.2 = (bf16[32,4,3584]{2,1,0:T(4,128)(2,1)}, bf16[32,4,3584]{2,1,0:T(4,128)(2,1)S(1)}, u32[]{:S(2)}, u32[]{:S(2)}) collective-permute-start(bf16[32,4,3584]{2,1,0:T(4,128)(2,1)} %maximum_select_fusion.1), channel_id=1, source_target_pairs={{0,4},{1,5},{2,6},{3,7},{4,0},{5,1},{6,2},{7,3},{8,12},{9,13},{10,... | collective-permute-start | bytes 2752520 | tf_op jit(solution)/shard_map/ppermute | solution.py:16
  60.2 0.9 copy-start.5
  61.1 3.5 %copy-start.6 = (bf16[128,3584]{1,0:T(8,128)(2,1)S(1)}, bf16[128,3584]{1,0:T(8,128)(2,1)}, u32[]{:S(2)}) copy-start(bf16[128,3584]{1,0:T(8,128)(2,1)} %maximum_select_fusion.2) | copy-start | bytes 2752516
  70.5 8.0 %copy-start.9 = (bf16[64,64]{1,0:T(8,128)(2,1)S(1)}, bf16[64,64]{1,0:T(8,128)(2,1)}, u32[]{:S(2)}) copy-start(bf16[64,64]{1,0:T(8,128)(2,1)} %param.19) | copy-start | bytes 24580
  70.5 60.8 %copy-start.7 = (bf16[64,4096]{1,0:T(8,128)(2,1)S(1)}, bf16[64,4096]{1,0:T(8,128)(2,1)}, u32[]{:S(2)}) copy-start(bf16[64,4096]{1,0:T(8,128)(2,1)} %param.16) | copy-start | bytes 1572868
  72.1 95.4 %all-to-all-start.1 = ((bf16[32,4,7168]{2,1,0:T(4,128)(2,1)}), bf16[32,4,7168]{2,1,0:T(4,128)(2,1)}, u32[]{:S(2)}, u32[]{:S(2)}) async-start(bf16[32,4,7168]{2,1,0:T(4,128)(2,1)} %convert_element_type.91), calls=%async_computation.1 | async-start | bytes 3670016 | tf_op jit(solution)/shard_map/all_to_all | solution.py:128
  78.5 56.6 %copy-start.2 = (bf16[32,512,128]{2,1,0:T(8,128)(2,1)S(1)}, bf16[32,512,128]{2,1,0:T(8,128)(2,1)}, u32[]{:S(2)}) copy-start(bf16[32,512,128]{2,1,0:T(8,128)(2,1)} %param.20) | copy-start | bytes 12582916
  135.1 1.6 copy-start.8
  144.9 1.2 copy-start.3
  147.5 1.3 copy-start.11
  157.1 1.2 copy-start.4
  159.7 1.4 copy-start.12
  161.2 4.0 %copy-start.10 = (bf16[32,512,128]{2,1,0:T(8,128)(2,1)S(1)}, bf16[32,512,128]{2,1,0:T(8,128)(2,1)}, u32[]{:S(2)}) copy-start(bf16[32,512,128]{2,1,0:T(8,128)(2,1)} %param.21) | copy-start | bytes 12582916
  161.2 4.7 %copy-start.13 = (f32[32,32,512]{2,1,0:T(8,128)S(1)}, f32[32,32,512]{2,1,0:T(8,128)}, u32[]{:S(2)}) copy-start(f32[32,32,512]{2,1,0:T(8,128)} %copy-done.12) | copy-start | bytes 6291460
  165.9 8.4 %copy-start.1 = (bf16[128,7168]{1,0:T(8,128)(2,1)S(1)}, bf16[128,7168]{1,0:T(8,128)(2,1)}, u32[]{:S(2)}) copy-start(bf16[128,7168]{1,0:T(8,128)(2,1)} %param.22) | copy-start | bytes 5505028
Sparse Core Ops, SparseCore 0:
  38.3 37.3 all-gather.1
where the time goes:
time: 182 us; the launch traced here: 181 us
  blocking collectives  66.7 us (37%)
  matrix products  42.3 us (23%)
  waiting for transfers between devices  27 us (15%)
  between operations  14.3 us (8%)
  other arithmetic  11.9 us (7%)
  starting transfers between devices  9.9 us (5%)
  local copies, waits for them, and re-layouts  9 us (5%)
    all_gather x1, blocking collectives, attention(): lax.all_gather(key_rope, 'ctx', axis=0, tiled=True)  52.8 us
    ppermute x3, waiting for transfers between devices, swapped(): lax.ppermute(shard, axis, [(i, i ^ 1 << bit) for i in range(lax.axis_size...  26.9 us
    all_to_all x1, blocking collectives, experts_layer(): lax.all_to_all(blocks, ('ctx', 'sec'), split_axis=0, concat_axis=0, tiled...  13.9 us
    dot_general x2, matrix products, update(): jnp.einsum('uhc,pc->hup', latents, latent_keys, preferred_element_type=jn...  9.27 us
    dot_general x2, matrix products, update(): jnp.einsum('uhr,pr->hup', rotary, rotary_keys, preferred_element_type=jnp...  6.39 us
    all_to_all x1, starting transfers between devices, combine_back(): lax.all_to_all(partial_value.astype(jnp.bfloat16), ('ctx', 'sec'), split_...  6.35 us
    dot_general x1, matrix products, expert_block(): jnp.dot(hidden, down_weight, preferred_element_type=jnp.float32)  5.89 us
    unnamed x27, local copies, waits for them, and re-layouts  5.4 us
  transfers between devices with their start and end apart: 5, of which 3 were waited for; matrix products, arithmetic and copies ran while one was open for 25% of the time, Pallas kernels for 0%

commit v1 on v0

v1 whole, which is shorter than its diff:
```python
import functools

import jax
import jax.numpy as jnp
from jax import lax
from jax.experimental import pallas as pl
from jax.experimental.pallas import tpu as pltpu
from jax.sharding import PartitionSpec as P

CAP = 4
SPLIT = 8
CHUNKS = 4
MESH_ID = pl.DeviceIdType.MESH
F32 = jnp.float32
BF16 = jnp.bfloat16
NT = (((1,), (1,)), ((), ()))


def kernel(
    dims,
    ids_ref,
    gates_ref,
    klat_ref,
    krope_ref,
    tok_hbm,
    qn_hbm,
    qr_hbm,
    ku_hbm,
    vu_hbm,
    gw_hbm,
    uw_hbm,
    dw_hbm,
    att_ref,
    rout_ref,
    tok,
    qn,
    qr,
    ku,
    vu,
    gw,
    uw,
    dw,
    qcat,
    keys,
    kown,
    outg,
    zbuf,
    arr,
    part,
    r1,
    s1,
    r2,
    s2,
    r3,
    rbuf,
    resb,
    wmix,
    load_sem,
    ksend,
    krecv,
    zsend,
    zrecv,
    asend,
    arecv,
    rsend,
    rrecv,
    bsend,
    brecv,
):
    groups, n_sec, rows, heads, lat, ropew, nope, hb = dims
    slots = groups * CAP
    width = tok.shape[1]
    cw = width // CHUNKS
    half = width // 2
    tokens = tok.shape[0]
    ctx = lax.axis_index("ctx")
    sec = lax.axis_index("sec")
    me = ctx * n_sec + sec
    g = me // SPLIT
    m = lax.rem(me, SPLIT)
    bx = lax.rem(m, 2)
    bc = lax.rem(m // 2, 2)
    by = m // 4
    mx = m + 1 - 2 * bx
    mc = m + 2 - 4 * bc
    my = m + 4 - 8 * by

    def dev(group, member):
        index = group * SPLIT + member
        return (index // n_sec, lax.rem(index, n_sec))

    def rcopy(src, dst, ss, rs, target):
        return pltpu.make_async_remote_copy(
            src_ref=src, dst_ref=dst, send_sem=ss, recv_sem=rs,
            device_id=target, device_id_type=MESH_ID,
        )

    nx, nc, ny = dev(g, mx), dev(g, mc), dev(g, my)
    others = [lax.rem(g + step, groups) for step in range(1, groups)]

    barrier = pltpu.get_barrier_semaphore()
    for target in [nx, nc, ny] + [dev(o, m) for o in others]:
        pl.semaphore_signal(barrier, inc=1, device_id=target, device_id_type=MESH_ID)

    pairs = [
        (tok_hbm, tok), (qn_hbm, qn), (qr_hbm, qr), (ku_hbm, ku),
        (gw_hbm, gw), (uw_hbm, uw), (dw_hbm, dw), (vu_hbm, vu),
    ]
    loads = [pltpu.make_async_copy(a, b, load_sem.at[i]) for i, (a, b) in enumerate(pairs)]
    for load in loads:
        load.start()

    lanes = wmix.shape[1]
    lane = lax.broadcasted_iota(jnp.int32, (tokens, lanes), 1)
    slot = lane & (slots - 1)
    expert = slot // CAP
    matches = jnp.zeros((tokens, lanes), F32)
    gate = jnp.zeros((tokens, lanes), F32)
    for k in range(ids_ref.shape[1]):
        hit = ids_ref[:, k : k + 1] == expert
        matches = jnp.where(hit, 1.0, matches)
        gate = gate + jnp.where(hit, gates_ref[:, k : k + 1], 0.0)
    earlier = (
        lax.broadcasted_iota(jnp.int32, (tokens, tokens), 1)
        < lax.broadcasted_iota(jnp.int32, (tokens, tokens), 0)
    )
    rank = jnp.dot(
        jnp.where(earlier, 1.0, 0.0).astype(BF16), matches.astype(BF16), preferred_element_type=F32
    )
    chosen = jnp.where(rank == (slot & (CAP - 1)).astype(F32), matches, 0.0)
    weight = chosen * gate
    w1 = weight.astype(BF16).astype(F32)
    w2 = (weight - w1).astype(BF16).astype(F32)
    w3 = weight - w1 - w2
    wmix[...] = jnp.where(
        lane < slots, w1, jnp.where(lane < 2 * slots, w2, jnp.where(lane < 3 * slots, w3, 0.0))
    ).astype(BF16)
    picker = chosen[:, :128].T[:slots].astype(BF16)

    kown[:, :lat] = klat_ref[...]
    kown[:, lat:] = jnp.concatenate([krope_ref[...], krope_ref[...]], axis=1)

    loads[0].wait()

    @pl.loop(0, CHUNKS)
    def _(c):
        cols = pl.ds(pl.multiple_of(c * cw, cw), cw)
        picked = jnp.dot(picker, tok[:, cols], preferred_element_type=F32)
        for e in range(groups):
            outg[e, :, cols] = picked[e * CAP : (e + 1) * CAP].astype(BF16)

    pl.semaphore_wait(barrier, 3 + len(others))

    zc = []
    for i, o in enumerate(others):
        cp = rcopy(outg.at[o], zbuf.at[g], zsend.at[i], zrecv.at[g], dev(o, m))
        cp.start()
        zc.append(cp)
    kc = []
    for i, o in enumerate(others):
        cp = rcopy(kown, keys.at[ctx], ksend.at[i], krecv.at[ctx], dev(o, m))
        cp.start()
        kc.append(cp)
    zbuf[g] = outg[g]
    keys[ctx] = kown[...]

    loads[1].wait()
    loads[2].wait()
    loads[3].wait()

    @pl.loop(0, heads // 2)
    def _(p):
        rope = qr[:, pl.ds(pl.multiple_of(p * 2 * ropew, 2 * ropew), 2 * ropew)]
        low = lax.broadcasted_iota(jnp.int32, rope.shape, 1) < ropew
        for k in range(2):
            h = p * 2 + k
            q = qn[:, pl.ds(pl.multiple_of(h * nope, nope), nope)]
            latent = lax.dot_general(q, ku[h], NT, preferred_element_type=F32)
            place = pl.ds(pl.multiple_of(h * rows, rows), rows)
            qcat[place, :lat] = latent.astype(BF16)
            keep = low if k == 0 else jnp.logical_not(low)
            qcat[place, lat:] = jnp.where(keep, rope.astype(F32), 0.0).astype(BF16)

    def zwait(i, o):
        rcopy(outg.at[o], zbuf.at[o], zsend.at[i], zrecv.at[o], dev(o, m)).wait_recv()

    for i, o in enumerate(others):
        zwait(i, o)

    @pl.loop(0, CHUNKS)
    def _(c):
        cols = pl.ds(pl.multiple_of(c * cw, cw), cw)
        blocks = [zbuf[e, :, cols].astype(F32) for e in range(groups)]
        arr[m, :, cols] = jnp.concatenate(blocks, axis=0).astype(BF16)

    left, right = pl.ds(0, half), pl.ds(half, half)
    halves = (left, right)
    pending = []

    def spread(kind, member, h, target):
        piece = arr.at[member, :, halves[h]]
        cp = rcopy(piece, piece, asend.at[kind, h], arecv.at[member, h], target)
        cp.start()
        pending.append(cp)

    def arrive(member, h):
        piece = arr.at[member, :, halves[h]]
        rcopy(piece, piece, asend.at[0, h], arecv.at[member, h], nx).wait_recv()

    mxy = mx + my - m
    spread(0, m, 0, nx)
    spread(1, m, 1, ny)
    spread(0, m, 1, nx)
    spread(1, m, 0, ny)
    spread(2, m, 0, nc)
    spread(2, m, 1, nc)

    def kshard(group, member):
        return (group * SPLIT + member) // n_sec

    def kpass(kind, group, member, target):
        piece = keys.at[kshard(group, member)]
        cp = rcopy(piece, piece, ksend.at[len(others) + kind * groups + group],
                   krecv.at[kshard(group, member)], target)
        cp.start()
        pending.append(cp)

    def karrive(group, member):
        piece = keys.at[kshard(group, member)]
        rcopy(piece, piece, ksend.at[0], krecv.at[kshard(group, member)], nx).wait_recv()

    arrive(mx, 0)
    spread(3, mx, 0, ny)
    arrive(my, 1)
    spread(3, my, 1, nx)
    spread(4, mx, 0, nc)
    spread(5, my, 1, nc)
    arrive(mx, 1)
    spread(4, mx, 1, nc)
    arrive(my, 0)
    spread(5, my, 0, nc)
    kpass(0, g, m, ny)
    kpass(1, g, m, nc)
    for o in others:
        karrive(o, m)
        kpass(0, o, m, ny)
        kpass(1, o, m, nc)
    arrive(mxy, 0)
    spread(6, mxy, 0, nc)
    arrive(mxy, 1)
    spread(6, mxy, 1, nc)
    for o in [g] + others:
        karrive(o, my)
        kpass(2, o, my, nc)
    mcx, mcy = mx + mc - m, my + mc - m
    for member in (mc, mcx, mcy, mxy + mc - m):
        arrive(member, 0)
        arrive(member, 1)
    loads[4].wait()
    loads[5].wait()
    loads[6].wait()

    count = SPLIT * slots
    step_w = 512
    ff = gw.shape[1]

    def gate_up(k, acc):
        cols = pl.ds(pl.multiple_of(k * step_w, step_w), step_w)
        x = arr[:, :, cols].reshape(count, step_w)
        return (
            acc[0] + jnp.dot(x, gw[cols], preferred_element_type=F32),
            acc[1] + jnp.dot(x, uw[cols], preferred_element_type=F32),
        )

    zero = jnp.zeros((count, ff), F32)
    gate_act, up_act = lax.fori_loop(0, width // step_w, gate_up, (zero, zero))
    hidden = (gate_act / (1.0 + jnp.exp(-gate_act)) * up_act).astype(BF16)

    c1, c2, c3 = [], [], []
    for c in range(CHUNKS):
        value = jnp.dot(hidden, dw[:, c * cw : (c + 1) * cw], preferred_element_type=F32)
        part[c] = value.astype(BF16).reshape(2, 2, 2, slots, cw)
        cp = rcopy(part.at[c, :, 1 - bc], r1.at[c], rsend.at[0, c], rrecv.at[0, c], nc)
        cp.start()
        c1.append(cp)

    loads[7].wait()
    for o in [g] + others:
        karrive(o, mc)
        karrive(o, mcy)

    seq = keys.shape[0] * keys.shape[1]
    block = hb * rows
    scale = (nope + ropew) ** -0.5

    def attend(first, last):
        @pl.loop(first, last)
        def _(b):
            q = qcat[pl.ds(pl.multiple_of(b * block, block), block)]
            kk = keys[...].reshape(seq, keys.shape[2])
            score = lax.dot_general(q, kk, NT, preferred_element_type=F32) * scale
            place = ctx * rows + (
                lax.broadcasted_iota(jnp.int32, (block, seq), 0) & (rows - 1)
            )
            allowed = lax.broadcasted_iota(jnp.int32, (block, seq), 1) <= place
            score = jnp.where(allowed, score, -1e30)
            top = jnp.max(score, axis=1, keepdims=True)
            expo = jnp.exp(score - top)
            total = jnp.sum(expo, axis=1, keepdims=True)
            mixed = jnp.dot(expo.astype(BF16), kk[:, :lat], preferred_element_type=F32)
            mixed = (mixed / total).astype(BF16)
            for k in range(hb):
                h = b * hb + k
                value = jnp.dot(
                    mixed[k * rows : (k + 1) * rows], vu[h], preferred_element_type=F32
                )
                vdim = value.shape[1]
                att_ref[:, pl.ds(pl.multiple_of(h * vdim, vdim), vdim)] = value.astype(BF16)

    nb = heads // hb
    attend(0, nb // 4)

    for c in range(CHUNKS):
        c1[c].wait_recv()
        for a in range(2):
            for b in range(2):
                s1[c, a, b] = (part[c, a, bc, b].astype(F32) + r1[c, a, b].astype(F32)).astype(BF16)
        src = s1.at[c, :, 1 - bx] if c % 2 == 0 else s1.at[c, 1 - by]
        cp = rcopy(src, r2.at[c], rsend.at[1, c], rrecv.at[1, c], nx if c % 2 == 0 else ny)
        cp.start()
        c2.append(cp)

    attend(nb // 4, nb // 2)

    for c in range(CHUNKS):
        c2[c].wait_recv()
        for a in range(2):
            mine = s1[c, a, bx] if c % 2 == 0 else s1[c, by, a]
            s2[c, a] = (mine.astype(F32) + r2[c, a].astype(F32)).astype(BF16)
        keep = by if c % 2 == 0 else bx
        cp = rcopy(s2.at[c, 1 - keep], r3.at[c], rsend.at[2, c], rrecv.at[2, c],
                   ny if c % 2 == 0 else nx)
        cp.start()
        c3.append(cp)

    attend(nb // 2, nb // 2 + nb // 4)

    for c in range(CHUNKS):
        c3[c].wait_recv()
        keep = by if c % 2 == 0 else bx
        total = s2[c, keep].astype(F32) + r3[c].astype(F32)
        for e in range(groups):
            rbuf[e, :, c * cw : (c + 1) * cw] = total[e * CAP : (e + 1) * CAP].astype(BF16)

    bc_list = []
    for i, o in enumerate(others):
        cp = rcopy(rbuf.at[o], resb.at[g], bsend.at[i], brecv.at[g], dev(o, m))
        cp.start()
        bc_list.append(cp)
    resb[g] = rbuf[g]

    attend(nb // 2 + nb // 4, nb)

    for i, o in enumerate(others):
        rcopy(rbuf.at[o], resb.at[o], bsend.at[i], brecv.at[o], dev(o, m)).wait_recv()

    @pl.loop(0, CHUNKS)
    def _(c):
        cols = pl.ds(pl.multiple_of(c * cw, cw), cw)
        blocks = [resb[e, :, cols].astype(F32) for e in range(groups)]
        block_rows = jnp.concatenate(blocks, axis=0)
        tall = jnp.concatenate([block_rows] * (lanes // slots), axis=0).astype(BF16)
        rout_ref[:, cols] = jnp.dot(wmix[...], tall, preferred_element_type=F32).astype(BF16)

    for cp in zc + kc + pending + c1 + c2 + c3 + bc_list:
        cp.wait_send()


def local(n_ctx, n_sec, qn, qr, klat, krope, ku, vu, tok, ids, gates, gw, uw, dw):
    devices = n_ctx * n_sec
    groups = devices // SPLIT
    slots = groups * CAP
    rows = qn.shape[0]
    heads, lat, nope = ku.shape
    ropew = krope.shape[1]
    width = tok.shape[1]
    cw = width // CHUNKS
    kw = lat + 2 * ropew
    hb = 4 if n_ctx * rows <= 2048 else 1
    hb = min(hb, heads)
    lanes = -(-3 * slots // 128) * 128
    dims = (groups, n_sec, rows, heads, lat, ropew, nope, hb)
    v = pl.BlockSpec(memory_space=pltpu.VMEM)
    a = pl.BlockSpec(memory_space=pl.ANY)
    dma = pltpu.SemaphoreType.DMA
    att, rout = pl.pallas_call(
        functools.partial(kernel, dims),
        out_shape=(
            jax.ShapeDtypeStruct((rows, heads * vu.shape[2]), BF16),
            jax.ShapeDtypeStruct(tok.shape, BF16),
        ),
        in_specs=[v, v, v, v] + [a] * 8,
        out_specs=(v, v),
        scratch_shapes=[
            pltpu.VMEM(tok.shape, BF16),
            pltpu.VMEM(qn.shape, BF16),
            pltpu.VMEM(qr.shape, BF16),
            pltpu.VMEM(ku.shape, BF16),
            pltpu.VMEM(vu.shape, BF16),
            pltpu.VMEM(gw.shape, BF16),
            pltpu.VMEM(uw.shape, BF16),
            pltpu.VMEM(dw.shape, BF16),
            pltpu.VMEM((heads * rows, kw), BF16),
            pltpu.VMEM((n_ctx, rows, kw), BF16),
            pltpu.VMEM((rows, kw), BF16),
            pltpu.VMEM((groups, CAP, width), BF16),
            pltpu.VMEM((groups, CAP, width), BF16),
            pltpu.VMEM((SPLIT, slots, width), BF16),
            pltpu.VMEM((CHUNKS, 2, 2, 2, slots, cw), BF16),
            pltpu.VMEM((CHUNKS, 2, 2, slots, cw), BF16),
            pltpu.VMEM((CHUNKS, 2, 2, slots, cw), BF16),
            pltpu.VMEM((CHUNKS, 2, slots, cw), BF16),
            pltpu.VMEM((CHUNKS, 2, slots, cw), BF16),
            pltpu.VMEM((CHUNKS, slots, cw), BF16),
            pltpu.VMEM((groups, CAP, width), BF16),
            pltpu.VMEM((groups, CAP, width), BF16),
            pltpu.VMEM((tok.shape[0], lanes), BF16),
            dma((8,)),
            dma((groups - 1 + 3 * groups,)),
            dma((n_ctx,)),
            dma((groups,)),
            dma((groups,)),
            dma((7, 2)),
            dma((SPLIT, 2)),
            dma((3, CHUNKS)),
            dma((3, CHUNKS)),
            dma((groups,)),
            dma((groups,)),
        ],
        compiler_params=pltpu.CompilerParams(
            collective_id=0, has_side_effects=True, vmem_limit_bytes=67043328
        ),
    )(ids, gates, klat, krope, tok, qn, qr, ku, vu, gw, uw, dw)
    return att, rout


def solution(mesh):
    body = functools.partial(local, mesh.shape["ctx"], mesh.shape["sec"])
    both = ("ctx", "sec")
    return jax.shard_map(
        body,
        mesh=mesh,
        in_specs=(
            P("ctx", "sec"),
            P("ctx", "sec"),
            P("ctx", None),
            P("ctx", None),
            P("sec", None, None),
            P("sec", None, None),
            P(both, None),
            P(both, None),
            P(both, None),
            P(None, both),
            P(None, both),
            P(both, None),
        ),
        out_specs=(P("ctx", "sec"), P(both, None)),
        check_vma=False,
    )
```

time: 182 us -> 62.6 us (0.34)
  the two profiles are of different devices: /device:TPU:11 before, /device:TPU:0 now
where the time goes in v1:
time: 62.6 us; the launch traced here: 62.3 us
  Pallas kernels  54.1 us (86%)
  local copies, waits for them, and re-layouts  7.54 us (12%)
  between operations  0.64 us (1%)
    pallas_call x1, Pallas kernels, local(): pl.pallas_call(functools.partial(kernel, dims), out_shape=(jax.ShapeDtype...  54.1 us
    unnamed x4, local copies, waits for them, and re-layouts  7.54 us

profile of v1, /device:TPU:0, one launch (start us, length us, event | category | flops | bytes accessed | tf_op | source)
XLA Modules:
  0.0 62.3 jit_solution(12973673047472892130)
XLA Ops:
  0.6 1.4 %copy.14.ids_ref = s32[128,8]{1,0:T(8,128)} copy(s32[128,8]{0,1:T(8,128)} %param.19) | data formatting | bytes 8192 | tf_op args[7]
  2.0 1.4 %copy.15.gates_ref = f32[128,8]{1,0:T(8,128)} copy(f32[128,8]{0,1:T(8,128)} %param.20) | data formatting | bytes 8192 | tf_op args[8]
  3.5 54.1 %shard_map.131 = (bf16[64,4096]{1,0:T(8,128)(2,1)}, bf16[128,7168]{1,0:T(8,128)(2,1)}) custom-call(s32[128,8]{1,0:T(8,128)} %copy.14.ids_ref, f32[128,8]{1,0:T(8,128)} %copy.15.gates_ref, bf16[64,512]{1,0:T(8,128)(2,1)} %klat_ref.1, bf16[64,64]{1,0:T(8,128)(2,1)} %krope_ref.1, bf16[128,7168]{1,0:T(8,128)(2,1)} %tok_hbm.1, bf16[64,4096]{1,0:T(8,128)(2,1)} %qn_hbm.1, ...), custom_call_target="tpu_custom_call" | custom-call | tf_op jit(solution)/shard_map/pallas_call | solution.py:396
  57.6 1.9 %copy.18 = bf16[64,4096]{1,0:T(8,128)(2,1)} copy(bf16[64,4096]{1,0:T(8,128)(2,1)} %get-tuple-element.4) | data formatting | bytes 1048576
  59.4 2.8 %copy.19 = bf16[128,7168]{1,0:T(8,128)(2,1)} copy(bf16[128,7168]{1,0:T(8,128)(2,1)} %get-tuple-element.5) | data formatting | bytes 3670016

commit v2 on v1

v2 whole, which is shorter than its diff:
```python
import functools

import jax
import jax.numpy as jnp
from jax import lax
from jax.experimental import pallas as pl
from jax.experimental.pallas import tpu as pltpu
from jax.sharding import PartitionSpec as P

CAP = 4
SPLIT = 8
CHUNKS = 4
LOG2E = 1.4426950408889634
MESH_ID = pl.DeviceIdType.MESH
F32 = jnp.float32
BF16 = jnp.bfloat16
NT = (((1,), (1,)), ((), ()))


def kernel(
    dims,
    ids_ref,
    gates_ref,
    klat_ref,
    krope_ref,
    tok_hbm,
    qn_hbm,
    qr_hbm,
    ku_hbm,
    vu_hbm,
    gw_hbm,
    uw_hbm,
    dw_hbm,
    att_ref,
    resb,
    wmix,
    tok,
    qn,
    qr,
    ku,
    vu,
    gw,
    uw,
    dw,
    qcat,
    keys,
    outg,
    zbuf,
    arr,
    acc,
    part,
    r1,
    s1,
    r2,
    s2,
    r3,
    rbuf,
    load_sem,
    kz_send,
    kx_send,
    ky_send,
    kc_send,
    krecv,
    zsend,
    zrecv,
    asend,
    arecv,
    rsend,
    rrecv,
    bsend,
    brecv,
):
    groups, n_sec, rows, heads, lat, ropew, nope, hb = dims
    slots = groups * CAP
    width = tok.shape[1]
    cw = width // CHUNKS
    tokens = tok.shape[0]
    sent = lat + 2 * ropew
    ctx = lax.axis_index("ctx")
    sec = lax.axis_index("sec")
    me = ctx * n_sec + sec
    g = me // SPLIT
    m = lax.rem(me, SPLIT)
    bx = lax.rem(m, 2)
    bc = lax.rem(m // 2, 2)
    by = m // 4
    mx = m + 1 - 2 * bx
    mc = m + 2 - 4 * bc
    my = m + 4 - 8 * by
    mxy = mx + my - m

    def dev(group, member):
        index = group * SPLIT + member
        return (index // n_sec, lax.rem(index, n_sec))

    pending = []

    def rcopy(src, dst, ss, rs, target):
        return pltpu.make_async_remote_copy(
            src_ref=src, dst_ref=dst, send_sem=ss, recv_sem=rs,
            device_id=target, device_id_type=MESH_ID,
        )

    def send(src, dst, ss, rs, target):
        cp = rcopy(src, dst, ss, rs, target)
        cp.start()
        pending.append(cp)
        return cp

    nx, nc, ny = dev(g, mx), dev(g, mc), dev(g, my)
    others = [lax.rem(g + step, groups) for step in range(1, groups)]
    every = [g] + others

    barrier = pltpu.get_barrier_semaphore()
    for target in [nx, nc, ny] + [dev(o, m) for o in others]:
        pl.semaphore_signal(barrier, inc=1, device_id=target, device_id_type=MESH_ID)

    pairs = [
        (tok_hbm, tok), (qn_hbm, qn), (qr_hbm, qr), (ku_hbm, ku),
        (gw_hbm, gw), (uw_hbm, uw), (dw_hbm, dw), (vu_hbm, vu),
    ]
    loads = [pltpu.make_async_copy(a, b, load_sem.at[i]) for i, (a, b) in enumerate(pairs)]
    for load in loads:
        load.start()

    lanes = wmix.shape[1]
    row = lax.broadcasted_iota(jnp.int32, (lanes, tokens), 0)
    slot = row & (slots - 1)
    expert = slot // CAP
    matches = jnp.zeros((lanes, tokens), F32)
    gate = jnp.zeros((lanes, tokens), F32)
    for k in range(ids_ref.shape[0]):
        hit = ids_ref[k : k + 1, :] == expert
        matches = jnp.where(hit, 1.0, matches)
        gate = gate + jnp.where(hit, gates_ref[k : k + 1, :], 0.0)
    earlier = (
        lax.broadcasted_iota(jnp.int32, (tokens, tokens), 0)
        < lax.broadcasted_iota(jnp.int32, (tokens, tokens), 1)
    )
    rank = jnp.dot(
        matches.astype(BF16), jnp.where(earlier, 1.0, 0.0).astype(BF16), preferred_element_type=F32
    )
    chosen = jnp.where(rank == (slot & (CAP - 1)).astype(F32), matches, 0.0)
    picker = chosen[:slots].astype(BF16)

    own_keys = keys.at[ctx]
    own_keys[:, :lat] = klat_ref[...]
    own_keys[:, lat:sent] = jnp.concatenate([krope_ref[...], krope_ref[...]], axis=1)

    loads[0].wait()
    for c in range(CHUNKS):
        picked = jnp.dot(picker, tok[:, c * cw : (c + 1) * cw], preferred_element_type=F32)
        for e in range(groups):
            outg[c, e] = picked[e * CAP : (e + 1) * CAP].astype(BF16)
        if c == 0:
            pl.semaphore_wait(barrier, 3 + len(others))
        for i, o in enumerate(others):
            send(outg.at[c, o], zbuf.at[c, g], zsend.at[c, i], zrecv.at[c, g], dev(o, m))

    part_rows = rows // 2

    def kpiece(shard, which):
        return keys.at[shard, pl.ds(pl.multiple_of(which * part_rows, part_rows), part_rows), pl.ds(0, sent)]

    def kwhole(shard):
        return keys.at[shard, :, pl.ds(0, sent)]

    def kshard(group, member):
        return (group * SPLIT + member) // n_sec

    def ksend(group, member, sem, target):
        shard = kshard(group, member)
        piece = kpiece(shard, bx)
        send(piece, piece, sem, krecv.at[shard, bx], target)

    def karrive(group, member, which):
        shard = kshard(group, member)
        piece = kpiece(shard, which)
        rcopy(piece, piece, kz_send.at[0], krecv.at[shard, which], nx).wait_recv()

    for i, o in enumerate(others):
        ksend(g, m, kz_send.at[i], dev(o, m))

    weight = chosen * gate
    w1 = weight.astype(BF16).astype(F32)
    w2 = (weight - w1).astype(BF16).astype(F32)
    w3 = weight - w1 - w2
    wmix[...] = jnp.where(
        row < slots, w1, jnp.where(row < 2 * slots, w2, jnp.where(row < 3 * slots, w3, 0.0))
    ).T.astype(BF16)

    maskw = keys.shape[2] - sent

    @pl.loop(0, keys.shape[0])
    def _(shard):
        key_place = shard * rows + lax.broadcasted_iota(jnp.int32, (rows, maskw), 0)
        query = lax.broadcasted_iota(jnp.int32, (rows, maskw), 1)
        hidden_key = (key_place > ctx * rows + query) & (query < rows)
        keys[shard, :, sent:] = jnp.where(hidden_key, -1e30, 0.0).astype(BF16)

    loads[1].wait()
    loads[2].wait()
    loads[3].wait()
    unit = jnp.where(
        lax.broadcasted_iota(jnp.int32, (rows, maskw), 0)
        == lax.broadcasted_iota(jnp.int32, (rows, maskw), 1),
        1.0,
        0.0,
    ).astype(BF16)

    def query_latents(first, last):
        @pl.loop(first, last)
        def _(p):
            rope = qr[:, pl.ds(pl.multiple_of(p * 2 * ropew, 2 * ropew), 2 * ropew)]
            low = lax.broadcasted_iota(jnp.int32, rope.shape, 1) < ropew
            for k in range(2):
                h = p * 2 + k
                q = qn[:, pl.ds(pl.multiple_of(h * nope, nope), nope)]
                latent = lax.dot_general(q, ku[h], NT, preferred_element_type=F32)
                place = pl.ds(pl.multiple_of(h * rows, rows), rows)
                qcat[place, :lat] = latent.astype(BF16)
                keep = low if k == 0 else jnp.logical_not(low)
                qcat[place, lat:sent] = jnp.where(keep, rope.astype(F32), 0.0).astype(BF16)
                qcat[place, sent:] = unit

    half_pairs = heads // 4
    query_latents(0, half_pairs)

    def spread(kind, member, c, target):
        piece = arr.at[c, member]
        send(piece, piece, asend.at[kind, c], arecv.at[c, member], target)

    def arrive(member, c):
        piece = arr.at[c, member]
        rcopy(piece, piece, asend.at[0, c], arecv.at[c, member], nx).wait_recv()

    def start_chunk(c):
        for i, o in enumerate(others):
            rcopy(outg.at[c, o], zbuf.at[c, o], zsend.at[c, i], zrecv.at[c, o], dev(o, m)).wait_recv()
        zbuf[c, g] = outg[c, g]
        blocks = [zbuf[c, e].astype(F32) for e in range(groups)]
        arr[c, m] = jnp.concatenate(blocks, axis=0).astype(BF16)
        spread(0, m, c, nx)
        spread(1, m, c, ny)
        spread(2, m, c, nc)

    def forward_chunk(c):
        arrive(mx, c)
        if c % 2 == 0:
            spread(3, mx, c, ny)
        spread(4, mx, c, nc)
        arrive(my, c)
        if c % 2 == 1:
            spread(3, my, c, nx)
        spread(5, my, c, nc)

    count = SPLIT * slots

    def finish_chunk(c):
        arrive(mxy, c)
        spread(6, mxy, c, nc)

    def gate_up(c):
        for member in (mc, mx + mc - m, my + mc - m, mxy + mc - m):
            arrive(member, c)
        x = arr[c].reshape(count, cw)
        g_part = jnp.dot(x, gw[c * cw : (c + 1) * cw], preferred_element_type=F32)
        u_part = jnp.dot(x, uw[c * cw : (c + 1) * cw], preferred_element_type=F32)
        if c == 0:
            acc[0] = g_part
            acc[1] = u_part
        else:
            acc[0] += g_part
            acc[1] += u_part

    start_chunk(0)
    start_chunk(1)
    forward_chunk(0)
    start_chunk(2)
    forward_chunk(1)
    start_chunk(3)
    finish_chunk(0)
    forward_chunk(2)
    finish_chunk(1)
    forward_chunk(3)

    ksend(g, m, ky_send.at[0], ny)
    for i, o in enumerate(others):
        karrive(o, m, bx)
        ksend(o, m, kx_send.at[i, 0], nx)
        ksend(o, m, ky_send.at[i + 1], ny)

    loads[4].wait()
    loads[5].wait()
    gate_up(0)
    finish_chunk(2)
    gate_up(1)
    finish_chunk(3)
    query_latents(half_pairs, heads // 2)
    gate_up(2)
    gate_up(3)
    gate_act = acc[0]
    hidden = (gate_act / (1.0 + jnp.exp(-gate_act)) * acc[1]).astype(BF16)

    c1, c2, c3 = [], [], []
    loads[6].wait()

    def down(c):
        value = jnp.dot(hidden, dw[:, c * cw : (c + 1) * cw], preferred_element_type=F32)
        part[c] = value.astype(BF16).reshape(2, 2, 2, slots, cw)
        c1.append(send(part.at[c, :, 1 - bc], r1.at[c], rsend.at[0, c], rrecv.at[0, c], nc))

    def sum_cores(c):
        c1[c].wait_recv()
        for a in range(2):
            for b in range(2):
                s1[c, a, b] = (part[c, a, bc, b].astype(F32) + r1[c, a, b].astype(F32)).astype(BF16)
        src = s1.at[c, :, 1 - bx] if c % 2 == 0 else s1.at[c, 1 - by]
        c2.append(send(src, r2.at[c], rsend.at[1, c], rrecv.at[1, c], nx if c % 2 == 0 else ny))

    def sum_first(c):
        c2[c].wait_recv()
        for a in range(2):
            mine = s1[c, a, bx] if c % 2 == 0 else s1[c, by, a]
            s2[c, a] = (mine.astype(F32) + r2[c, a].astype(F32)).astype(BF16)
        keep = by if c % 2 == 0 else bx
        c3.append(send(s2.at[c, 1 - keep], r3.at[c], rsend.at[2, c], rrecv.at[2, c],
                       ny if c % 2 == 0 else nx))

    def sum_second(c):
        c3[c].wait_recv()
        keep = by if c % 2 == 0 else bx
        total = s2[c, keep].astype(F32) + r3[c].astype(F32)
        for e in range(groups):
            rbuf[c, e] = total[e * CAP : (e + 1) * CAP].astype(BF16)
        for i, o in enumerate(others):
            send(rbuf.at[c, o], resb.at[c, g], bsend.at[c, i], brecv.at[c, g], dev(o, m))
        resb[c, g] = rbuf[c, g]

    down(0)
    down(1)
    down(2)
    sum_cores(0)
    down(3)
    sum_cores(1)
    sum_cores(2)
    sum_cores(3)

    for i, o in enumerate(every):
        karrive(o, my, bx)
        ksend(o, my, kx_send.at[i, 1], nx)
    shard = kshard(g, m)
    send(kwhole(shard), kwhole(shard), kc_send.at[0, 0], krecv.at[kshard(g, m), 0], nc)
    for i, o in enumerate(others):
        karrive(o, m, 1 - bx)
        shard = kshard(o, m)
        send(kwhole(shard), kwhole(shard), kc_send.at[i + 1, 0], krecv.at[shard, 0], nc)
    sum_first(0)
    sum_first(1)
    for i, o in enumerate(every):
        karrive(o, my, 1 - bx)
        shard = kshard(o, my)
        send(kwhole(shard), kwhole(shard), kc_send.at[i, 1], krecv.at[shard, 0], nc)
    loads[7].wait()
    for o in every:
        for member in (mc, my + mc - m):
            shard = kshard(o, member)
            rcopy(kwhole(shard), kwhole(shard), kc_send.at[0, 0], krecv.at[shard, 0], nc).wait_recv()

    seq = keys.shape[0] * keys.shape[1]
    block = hb * rows
    scale = (nope + ropew) ** -0.5 * LOG2E

    def attend(first, last):
        @pl.loop(first, last)
        def _(b):
            q = qcat[pl.ds(pl.multiple_of(b * block, block), block)]
            kk = keys[...].reshape(seq, keys.shape[2])
            score = lax.dot_general(q, kk, NT, preferred_element_type=F32)
            top = jnp.max(score, axis=1, keepdims=True)
            expo = jnp.exp2((score - top) * scale)
            total = jnp.sum(expo, axis=1, keepdims=True)
            mixed = jnp.dot(expo.astype(BF16), kk[:, :lat], preferred_element_type=F32)
            mixed = (mixed / total).astype(BF16)
            for k in range(hb):
                h = b * hb + k
                value = jnp.dot(
                    mixed[k * rows : (k + 1) * rows], vu[h], preferred_element_type=F32
                )
                vdim = value.shape[1]
                att_ref[:, pl.ds(pl.multiple_of(h * vdim, vdim), vdim)] = value.astype(BF16)

    nb = heads // hb
    eighth = nb // 8
    sum_first(2)
    sum_first(3)
    attend(0, eighth)
    sum_second(0)
    sum_second(1)
    attend(eighth, 2 * eighth)
    sum_second(2)
    sum_second(3)
    attend(2 * eighth, nb)

    for c in range(CHUNKS):
        for i, o in enumerate(others):
            rcopy(rbuf.at[c, o], resb.at[c, o], bsend.at[c, i], brecv.at[c, o], dev(o, m)).wait_recv()
    for cp in pending:
        cp.wait_send()


def finish(res_ref, wmix_ref, att_in, rout_ref, att_out):
    groups = res_ref.shape[1]
    block_rows = jnp.concatenate([res_ref[0, e].astype(F32) for e in range(groups)], axis=0)
    times = wmix_ref.shape[1] // block_rows.shape[0]
    tall = jnp.concatenate([block_rows] * times, axis=0).astype(BF16)
    rout_ref[...] = jnp.dot(wmix_ref[...], tall, preferred_element_type=F32).astype(BF16)
    att_out[...] = att_in[...]


def local(n_ctx, n_sec, qn, qr, klat, krope, ku, vu, tok, ids, gates, gw, uw, dw):
    devices = n_ctx * n_sec
    groups = devices // SPLIT
    slots = groups * CAP
    rows = qn.shape[0]
    heads, lat, nope = ku.shape
    ropew = krope.shape[1]
    tokens, width = tok.shape
    cw = width // CHUNKS
    kw = lat + 2 * ropew + 128
    hb = 4 if n_ctx * rows <= 2048 else 1
    lanes = -(-3 * slots // 128) * 128
    dims = (groups, n_sec, rows, heads, lat, ropew, nope, hb)
    v = pl.BlockSpec(memory_space=pltpu.VMEM)
    a = pl.BlockSpec(memory_space=pl.ANY)
    dma = pltpu.SemaphoreType.DMA
    out_width = heads * vu.shape[2]
    att, res, wmix = pl.pallas_call(
        functools.partial(kernel, dims),
        out_shape=(
            jax.ShapeDtypeStruct((rows, out_width), BF16),
            jax.ShapeDtypeStruct((CHUNKS, groups, CAP, cw), BF16),
            jax.ShapeDtypeStruct((tokens, lanes), BF16),
        ),
        in_specs=[v, v, v, v] + [a] * 8,
        out_specs=(v, v, v),
        scratch_shapes=[
            pltpu.VMEM(tok.shape, BF16),
            pltpu.VMEM(qn.shape, BF16),
            pltpu.VMEM(qr.shape, BF16),
            pltpu.VMEM(ku.shape, BF16),
            pltpu.VMEM(vu.shape, BF16),
            pltpu.VMEM(gw.shape, BF16),
            pltpu.VMEM(uw.shape, BF16),
            pltpu.VMEM(dw.shape, BF16),
            pltpu.VMEM((heads * rows, kw), BF16),
            pltpu.VMEM((n_ctx, rows, kw), BF16),
            pltpu.VMEM((CHUNKS, groups, CAP, cw), BF16),
            pltpu.VMEM((CHUNKS, groups, CAP, cw), BF16),
            pltpu.VMEM((CHUNKS, SPLIT, slots, cw), BF16),
            pltpu.VMEM((2, SPLIT * slots, gw.shape[1]), F32),
            pltpu.VMEM((CHUNKS, 2, 2, 2, slots, cw), BF16),
            pltpu.VMEM((CHUNKS, 2, 2, slots, cw), BF16),
            pltpu.VMEM((CHUNKS, 2, 2, slots, cw), BF16),
            pltpu.VMEM((CHUNKS, 2, slots, cw), BF16),
            pltpu.VMEM((CHUNKS, 2, slots, cw), BF16),
            pltpu.VMEM((CHUNKS, slots, cw), BF16),
            pltpu.VMEM((CHUNKS, groups, CAP, cw), BF16),
            dma((8,)),
            dma((groups,)),
            dma((groups, 2)),
            dma((groups,)),
            dma((groups, 2)),
            dma((n_ctx, 2)),
            dma((CHUNKS, groups)),
            dma((CHUNKS, groups)),
            dma((7, CHUNKS)),
            dma((CHUNKS, SPLIT)),
            dma((3, CHUNKS)),
            dma((3, CHUNKS)),
            dma((CHUNKS, groups)),
            dma((CHUNKS, groups)),
        ],
        compiler_params=pltpu.CompilerParams(
            collective_id=0, has_side_effects=True, vmem_limit_bytes=67043328
        ),
    )(ids.T, gates.T, klat, krope, tok, qn, qr, ku, vu, gw, uw, dw)
    rout, att = pl.pallas_call(
        finish,
        grid=(CHUNKS,),
        out_shape=(jax.ShapeDtypeStruct(tok.shape, BF16), jax.ShapeDtypeStruct(att.shape, BF16)),
        in_specs=[
            pl.BlockSpec((1, groups, CAP, cw), lambda i: (i, 0, 0, 0)),
            pl.BlockSpec((tokens, lanes), lambda i: (0, 0)),
            pl.BlockSpec((rows, out_width // CHUNKS), lambda i: (0, i)),
        ],
        out_specs=(
            pl.BlockSpec((tokens, cw), lambda i: (0, i)),
            pl.BlockSpec((rows, out_width // CHUNKS), lambda i: (0, i)),
        ),
    )(res, wmix, att)
    return att, rout


def solution(mesh):
    body = functools.partial(local, mesh.shape["ctx"], mesh.shape["sec"])
    both = ("ctx", "sec")
    return jax.shard_map(
        body,
        mesh=mesh,
        in_specs=(
            P("ctx", "sec"),
            P("ctx", "sec"),
            P("ctx", None),
            P("ctx", None),
            P("sec", None, None),
            P("sec", None, None),
            P(both, None),
            P(both, None),
            P(both, None),
            P(None, both),
            P(None, both),
            P(both, None),
        ),
        out_specs=(P("ctx", "sec"), P(both, None)),
        check_vma=False,
    )
```

time: 62.6 us -> 57.2 us (0.914)
  local copies, waits for them, and re-layouts: 7.54 us -> 0 us
  Pallas kernels: 54.1 us -> 56.3 us
    unnamed x4 -> x0, local copies, waits for them, and re-layouts: 7.54 us -> none
    pallas_call x0 -> x1, Pallas kernels: none -> 4.01 us  [local(): pl.pallas_call(finish, grid=(CHUNKS,), out_shape=(jax.ShapeDtypeStruct(to...]
    pallas_call x1, Pallas kernels: 54.1 us -> 52.3 us  [local(): pl.pallas_call(functools.partial(kernel, dims), out_shape=(jax.ShapeDtype...]
where the time goes in v2:
time: 57.2 us; the launch traced here: 56.9 us
  Pallas kernels  56.3 us (98%)
  between operations  0.64 us (1%)
    pallas_call x1, Pallas kernels, local(): pl.pallas_call(functools.partial(kernel, dims), out_shape=(jax.ShapeDtype...  52.3 us
    pallas_call x1, Pallas kernels, local(): pl.pallas_call(finish, grid=(CHUNKS,), out_shape=(jax.ShapeDtypeStruct(to...  4.01 us

profile of v2, /device:TPU:0, one launch (start us, length us, event | category | flops | bytes accessed | tf_op | source)
XLA Modules:
  0.0 56.9 jit_solution(408007182767139392)
XLA Ops:
  0.6 52.3 %shard_map.131 = (bf16[64,4096]{1,0:T(8,128)(2,1)}, bf16[4,4,4,1792]{3,2,1,0:T(4,128)(2,1)}, bf16[128,128]{1,0:T(8,128)(2,1)}) custom-call(s32[8,128]{1,0:T(8,128)} %bitcast.2, f32[8,128]{1,0:T(8,128)} %bitcast.3, bf16[64,512]{1,0:T(8,128)(2,1)} %klat_ref.1, bf16[64,64]{1,0:T(8,128)(2,1)} %krope_ref.1, bf16[128,7168]{1,0:T(8,128)(2,1)} %tok_hbm.1, ...), custom_call_target="tpu_custom_call" | custom-call | tf_op jit(solution)/shard_map/pallas_call | solution.py:438
  52.9 4.0 %shard_map.132 = (bf16[128,7168]{1,0:T(8,128)(2,1)}, bf16[64,4096]{1,0:T(8,128)(2,1)}) custom-call(bf16[4,4,4,1792]{3,2,1,0:T(4,128)(2,1)} %get-tuple-element.7.res_ref, bf16[128,128]{1,0:T(8,128)(2,1)} %get-tuple-element.8.wmix_ref, bf16[64,4096]{1,0:T(8,128)(2,1)} %get-tuple-element.9.att_in), custom_call_target="tpu_custom_call" | custom-call | tf_op jit(solution)/shard_map/pallas_call | solution.py:488

commit v3 on v2

--- a/solution.py
+++ b/solution.py
@@ -111,17 +111,56 @@
     others = [lax.rem(g + step, groups) for step in range(1, groups)]
     every = [g] + others
 
+    tok_loads = []
+    for c in range(CHUNKS):
+        cols = pl.ds(c * cw, cw)
+        tok_loads.append(
+            pltpu.make_async_copy(tok_hbm.at[:, cols], tok.at[:, cols], load_sem.at[8 + c])
+        )
+        tok_loads[c].start()
+
     barrier = pltpu.get_barrier_semaphore()
     for target in [nx, nc, ny] + [dev(o, m) for o in others]:
         pl.semaphore_signal(barrier, inc=1, device_id=target, device_id_type=MESH_ID)
 
     pairs = [
-        (tok_hbm, tok), (qn_hbm, qn), (qr_hbm, qr), (ku_hbm, ku),
+        (qn_hbm, qn), (qr_hbm, qr), (ku_hbm, ku),
         (gw_hbm, gw), (uw_hbm, uw), (dw_hbm, dw), (vu_hbm, vu),
     ]
-    loads = [pltpu.make_async_copy(a, b, load_sem.at[i]) for i, (a, b) in enumerate(pairs)]
-    for load in loads:
-        load.start()
+    loads = [None]
+    for i, (a, b) in enumerate(pairs):
+        loads.append(pltpu.make_async_copy(a, b, load_sem.at[i]))
+
+    own_keys = keys.at[ctx]
+    own_keys[:, :lat] = klat_ref[...]
+    own_keys[:, lat:sent] = jnp.concatenate([krope_ref[...], krope_ref[...]], axis=1)
+
+    pl.semaphore_wait(barrier, 3 + len(others))
+    part_rows = rows // 2
+
+    def kpiece(shard, which):
+        return keys.at[shard, pl.ds(pl.multiple_of(which * part_rows, part_rows), part_rows), pl.ds(0, sent)]
+
+    def kwhole(shard):
+        return keys.at[shard, :, pl.ds(0, sent)]
+
+    def kshard(group, member):
+        return (group * SPLIT + member) // n_sec
+
+    def ksend(group, member, which, sem, target):
+        shard = kshard(group, member)
+        piece = kpiece(shard, which)
+        send(piece, piece, sem, krecv.at[shard, which], target)
+
+    def karrive(group, member, which):
+        shard = kshard(group, member)
+        piece = kpiece(shard, which)
+        rcopy(piece, piece, kz_send.at[0], krecv.at[shard, which], nx).wait_recv()
+
+    for i, o in enumerate(others):
+        ksend(g, m, bx, kz_send.at[i], dev(o, m))
+    for which in range(2):
+        ksend(g, m, which, kz_send.at[groups - 1 + which], ny)
 
     lanes = wmix.shape[1]
     row = lax.broadcasted_iota(jnp.int32, (lanes, tokens), 0)
@@ -143,44 +182,16 @@
     chosen = jnp.where(rank == (slot & (CAP - 1)).astype(F32), matches, 0.0)
     picker = chosen[:slots].astype(BF16)
 
-    own_keys = keys.at[ctx]
-    own_keys[:, :lat] = klat_ref[...]
-    own_keys[:, lat:sent] = jnp.concatenate([krope_ref[...], krope_ref[...]], axis=1)
-
-    loads[0].wait()
-    for c in range(CHUNKS):
+    for c in range(CHUNKS):
+        tok_loads[c].wait()
         picked = jnp.dot(picker, tok[:, c * cw : (c + 1) * cw], preferred_element_type=F32)
         for e in range(groups):
             outg[c, e] = picked[e * CAP : (e + 1) * CAP].astype(BF16)
-        if c == 0:
-            pl.semaphore_wait(barrier, 3 + len(others))
         for i, o in enumerate(others):
             send(outg.at[c, o], zbuf.at[c, g], zsend.at[c, i], zrecv.at[c, g], dev(o, m))
 
-    part_rows = rows // 2
-
-    def kpiece(shard, which):
-        return keys.at[shard, pl.ds(pl.multiple_of(which * part_rows, part_rows), part_rows), pl.ds(0, sent)]
-
-    def kwhole(shard):
-        return keys.at[shard, :, pl.ds(0, sent)]
-
-    def kshard(group, member):
-        return (group * SPLIT + member) // n_sec
-
-    def ksend(group, member, sem, target):
-        shard = kshard(group, member)
-        piece = kpiece(shard, bx)
-        send(piece, piece, sem, krecv.at[shard, bx], target)
-
-    def karrive(group, member, which):
-        shard = kshard(group, member)
-        piece = kpiece(shard, which)
-        rcopy(piece, piece, kz_send.at[0], krecv.at[shard, which], nx).wait_recv()
-
-    for i, o in enumerate(others):
-        ksend(g, m, kz_send.at[i], dev(o, m))
-
+    for load in loads[1:4]:
+        load.start()
     weight = chosen * gate
     w1 = weight.astype(BF16).astype(F32)
     w2 = (weight - w1).astype(BF16).astype(F32)
@@ -201,6 +212,8 @@
     loads[1].wait()
     loads[2].wait()
     loads[3].wait()
+    for load in loads[4:]:
+        load.start()
     unit = jnp.where(
         lax.broadcasted_iota(jnp.int32, (rows, maskw), 0)
         == lax.broadcasted_iota(jnp.int32, (rows, maskw), 1),
@@ -226,6 +239,11 @@
     half_pairs = heads // 4
     query_latents(0, half_pairs)
 
+    for i, o in enumerate(others):
+        karrive(o, m, bx)
+        ksend(o, m, bx, kx_send.at[i, 0], nx)
+        ksend(o, m, bx, ky_send.at[i], ny)
+
     def spread(kind, member, c, target):
         piece = arr.at[c, member]
         send(piece, piece, asend.at[kind, c], arecv.at[c, member], target)
@@ -275,6 +293,9 @@
 
     start_chunk(0)
     start_chunk(1)
+    for i, o in enumerate(others):
+        karrive(o, my, bx)
+        ksend(o, my, bx, kx_send.at[i, 1], nx)
     forward_chunk(0)
     start_chunk(2)
     forward_chunk(1)
@@ -284,11 +305,18 @@
     finish_chunk(1)
     forward_chunk(3)
 
-    ksend(g, m, ky_send.at[0], ny)
+    shard = kshard(g, m)
+    send(kwhole(shard), kwhole(shard), kc_send.at[0, 0], krecv.at[shard, 0], nc)
     for i, o in enumerate(others):
-        karrive(o, m, bx)
-        ksend(o, m, kx_send.at[i, 0], nx)
-        ksend(o, m, ky_send.at[i + 1], ny)
+        karrive(o, m, 1 - bx)
+        shard = kshard(o, m)
+        send(kwhole(shard), kwhole(shard), kc_send.at[i + 1, 0], krecv.at[shard, 0], nc)
+    for i, o in enumerate(every):
+        karrive(o, my, 1 - bx)
+        if i == 0:
+            karrive(o, my, bx)
+        shard = kshard(o, my)
+        send(kwhole(shard), kwhole(shard), kc_send.at[i, 1], krecv.at[shard, 0], nc)
 
     loads[4].wait()
     loads[5].wait()
@@ -337,30 +365,9 @@
             send(rbuf.at[c, o], resb.at[c, g], bsend.at[c, i], brecv.at[c, g], dev(o, m))
         resb[c, g] = rbuf[c, g]
 
-    down(0)
-    down(1)
-    down(2)
-    sum_cores(0)
-    down(3)
-    sum_cores(1)
-    sum_cores(2)
-    sum_cores(3)
-
-    for i, o in enumerate(every):
-        karrive(o, my, bx)
-        ksend(o, my, kx_send.at[i, 1], nx)
-    shard = kshard(g, m)
-    send(kwhole(shard), kwhole(shard), kc_send.at[0, 0], krecv.at[kshard(g, m), 0], nc)
-    for i, o in enumerate(others):
-        karrive(o, m, 1 - bx)
-        shard = kshard(o, m)
-        send(kwhole(shard), kwhole(shard), kc_send.at[i + 1, 0], krecv.at[shard, 0], nc)
-    sum_first(0)
-    sum_first(1)
-    for i, o in enumerate(every):
-        karrive(o, my, 1 - bx)
-        shard = kshard(o, my)
-        send(kwhole(shard), kwhole(shard), kc_send.at[i, 1], krecv.at[shard, 0], nc)
+    for c in range(CHUNKS):
+        down(c)
+
     loads[7].wait()
     for o in every:
         for member in (mc, my + mc - m):
@@ -392,15 +399,16 @@
 
     nb = heads // hb
     eighth = nb // 8
-    sum_first(2)
-    sum_first(3)
     attend(0, eighth)
-    sum_second(0)
-    sum_second(1)
-    attend(eighth, 2 * eighth)
-    sum_second(2)
-    sum_second(3)
-    attend(2 * eighth, nb)
+    for c in range(CHUNKS):
+        sum_cores(c)
+    attend(eighth, 3 * eighth)
+    for c in range(CHUNKS):
+        sum_first(c)
+    attend(3 * eighth, 5 * eighth)
+    for c in range(CHUNKS):
+        sum_second(c)
+    attend(5 * eighth, nb)
 
     for c in range(CHUNKS):
         for i, o in enumerate(others):
@@ -412,9 +420,11 @@
 def finish(res_ref, wmix_ref, att_in, rout_ref, att_out):
     groups = res_ref.shape[1]
     block_rows = jnp.concatenate([res_ref[0, e].astype(F32) for e in range(groups)], axis=0)
-    times = wmix_ref.shape[1] // block_rows.shape[0]
-    tall = jnp.concatenate([block_rows] * times, axis=0).astype(BF16)
-    rout_ref[...] = jnp.dot(wmix_ref[...], tall, preferred_element_type=F32).astype(BF16)
+    block_rows = block_rows.astype(BF16)
+    tall = jnp.concatenate([block_rows] * 3, axis=0)
+    rout_ref[...] = jnp.dot(
+        wmix_ref[:, : tall.shape[0]], tall, preferred_element_type=F32
+    ).astype(BF16)
     att_out[...] = att_in[...]
 
 
@@ -466,8 +476,8 @@
             pltpu.VMEM((CHUNKS, 2, slots, cw), BF16),
             pltpu.VMEM((CHUNKS, slots, cw), BF16),
             pltpu.VMEM((CHUNKS, groups, CAP, cw), BF16),
-            dma((8,)),
-            dma((groups,)),
+            dma((8 + CHUNKS,)),
+            dma((groups + 1,)),
             dma((groups, 2)),
             dma((groups,)),
             dma((groups, 2)),

time: 57.2 us -> 56 us (0.979)
  Pallas kernels: 56.3 us -> 55.1 us
    pallas_call x1, Pallas kernels: 52.3 us -> 51.2 us  [local(): pl.pallas_call(functools.partial(kernel, dims), out_shape=(jax.ShapeDtype...]
where the time goes in v3:
time: 56 us; the launch traced here: 55.8 us
  Pallas kernels  55.1 us (98%)
  between operations  0.64 us (1%)
    pallas_call x1, Pallas kernels, local(): pl.pallas_call(functools.partial(kernel, dims), out_shape=(jax.ShapeDtype...  51.2 us
    pallas_call x1, Pallas kernels, local(): pl.pallas_call(finish, grid=(CHUNKS,), out_shape=(jax.ShapeDtypeStruct(to...  3.96 us

profile of v3, /device:TPU:0, one launch (start us, length us, event | category | flops | bytes accessed | tf_op | source)
XLA Modules:
  0.0 55.8 jit_solution(12688495702139827964)
XLA Ops:
  0.6 51.2 %shard_map.131 = (bf16[64,4096]{1,0:T(8,128)(2,1)}, bf16[4,4,4,1792]{3,2,1,0:T(4,128)(2,1)}, bf16[128,128]{1,0:T(8,128)(2,1)}) custom-call(s32[8,128]{1,0:T(8,128)} %bitcast.2, f32[8,128]{1,0:T(8,128)} %bitcast.3, bf16[64,512]{1,0:T(8,128)(2,1)} %klat_ref.1, bf16[64,64]{1,0:T(8,128)(2,1)} %krope_ref.1, bf16[128,7168]{1,0:T(8,128)(2,1)} %tok_hbm.1, ...), custom_call_target="tpu_custom_call" | custom-call | tf_op jit(solution)/shard_map/pallas_call | solution.py:448
  51.8 4.0 %shard_map.132 = (bf16[128,7168]{1,0:T(8,128)(2,1)}, bf16[64,4096]{1,0:T(8,128)(2,1)}) custom-call(bf16[4,4,4,1792]{3,2,1,0:T(4,128)(2,1)} %get-tuple-element.7.res_ref, bf16[128,128]{1,0:T(8,128)(2,1)} %get-tuple-element.8.wmix_ref, bf16[64,4096]{1,0:T(8,128)(2,1)} %get-tuple-element.9.att_in), custom_call_target="tpu_custom_call" | custom-call | tf_op jit(solution)/shard_map/pallas_call | solution.py:498

commit v4 on v3

--- a/solution.py
+++ b/solution.py
@@ -418,14 +418,15 @@
 
 
 def finish(res_ref, wmix_ref, att_in, rout_ref, att_out):
-    groups = res_ref.shape[1]
-    block_rows = jnp.concatenate([res_ref[0, e].astype(F32) for e in range(groups)], axis=0)
-    block_rows = block_rows.astype(BF16)
-    tall = jnp.concatenate([block_rows] * 3, axis=0)
-    rout_ref[...] = jnp.dot(
-        wmix_ref[:, : tall.shape[0]], tall, preferred_element_type=F32
-    ).astype(BF16)
+    chunks, groups, _, cw = res_ref.shape
     att_out[...] = att_in[...]
+    for c in range(chunks):
+        blocks = [res_ref[c, e].astype(F32) for e in range(groups)]
+        block_rows = jnp.concatenate(blocks, axis=0).astype(BF16)
+        tall = jnp.concatenate([block_rows] * 3, axis=0)
+        rout_ref[:, c * cw : (c + 1) * cw] = jnp.dot(
+            wmix_ref[:, : tall.shape[0]], tall, preferred_element_type=F32
+        ).astype(BF16)
 
 
 def local(n_ctx, n_sec, qn, qr, klat, krope, ku, vu, tok, ids, gates, gw, uw, dw):
@@ -497,17 +498,9 @@
     )(ids.T, gates.T, klat, krope, tok, qn, qr, ku, vu, gw, uw, dw)
     rout, att = pl.pallas_call(
         finish,
-        grid=(CHUNKS,),
         out_shape=(jax.ShapeDtypeStruct(tok.shape, BF16), jax.ShapeDtypeStruct(att.shape, BF16)),
-        in_specs=[
-            pl.BlockSpec((1, groups, CAP, cw), lambda i: (i, 0, 0, 0)),
-            pl.BlockSpec((tokens, lanes), lambda i: (0, 0)),
-            pl.BlockSpec((rows, out_width // CHUNKS), lambda i: (0, i)),
-        ],
-        out_specs=(
-            pl.BlockSpec((tokens, cw), lambda i: (0, i)),
-            pl.BlockSpec((rows, out_width // CHUNKS), lambda i: (0, i)),
-        ),
+        in_specs=[v, v, v],
+        out_specs=(v, v),
     )(res, wmix, att)
     return att, rout
 

time: 56 us -> 55.2 us (0.986)
  Pallas kernels: 55.1 us -> 54.3 us
    pallas_call x1, Pallas kernels: 3.96 us -> 3.16 us  [local(): pl.pallas_call(finish, out_shape=(jax.ShapeDtypeStruct(tok.shape, BF16),...]
where the time goes in v4:
time: 55.2 us; the launch traced here: 55 us
  Pallas kernels  54.3 us (98%)
  between operations  0.64 us (1%)
    pallas_call x1, Pallas kernels, local(): pl.pallas_call(functools.partial(kernel, dims), out_shape=(jax.ShapeDtype...  51.2 us
    pallas_call x1, Pallas kernels, local(): pl.pallas_call(finish, out_shape=(jax.ShapeDtypeStruct(tok.shape, BF16),...  3.16 us

profile of v4, /device:TPU:0, one launch (start us, length us, event | category | flops | bytes accessed | tf_op | source)
XLA Modules:
  0.0 55.0 jit_solution(14177206781001371796)
XLA Ops:
  0.6 51.2 %shard_map.131 = (bf16[64,4096]{1,0:T(8,128)(2,1)}, bf16[4,4,4,1792]{3,2,1,0:T(4,128)(2,1)}, bf16[128,128]{1,0:T(8,128)(2,1)}) custom-call(s32[8,128]{1,0:T(8,128)} %bitcast.2, f32[8,128]{1,0:T(8,128)} %bitcast.3, bf16[64,512]{1,0:T(8,128)(2,1)} %klat_ref.1, bf16[64,64]{1,0:T(8,128)(2,1)} %krope_ref.1, bf16[128,7168]{1,0:T(8,128)(2,1)} %tok_hbm.1, ...), custom_call_target="tpu_custom_call" | custom-call | tf_op jit(solution)/shard_map/pallas_call | solution.py:449
  51.8 3.2 %shard_map.132 = (bf16[128,7168]{1,0:T(8,128)(2,1)}, bf16[64,4096]{1,0:T(8,128)(2,1)}) custom-call(bf16[4,4,4,1792]{3,2,1,0:T(4,128)(2,1)} %get-tuple-element.7.res_ref, bf16[128,128]{1,0:T(8,128)(2,1)} %get-tuple-element.8.wmix_ref, bf16[64,4096]{1,0:T(8,128)(2,1)} %get-tuple-element.9.att_in), custom_call_target="tpu_custom_call" | custom-call | tf_op jit(solution)/shard_map/pallas_call | solution.py:499
